TPU v7x, 128 devices: a whole 4x4x4 slice. The times are simulated.
128 devices in a mesh: sub: 8 (over z, core), grp: 16 (over x, y).
Axes of the slice: x: 4, y: 4, z: 4, core: 2. Of those that a mesh axis runs over, the one named last changes fastest.
Arguments:
- schur: bfloat16 [512, 1024, 1024], P(('sub', 'grp')), as said below
- mortar: bfloat16 [512, 8, 128, 128], P(('sub', 'grp')), may hold values from -0.5 to 0.5
- partner: int32 [512, 4], P(('sub', 'grp')), may hold values from 0 to 15, as said below
- corner_map: int32 [512, 8], P(('sub', 'grp')), may hold values from 0 to 127
- coarse_inv: float32 [8, 128, 128], P('sub'), as said below
- load: float32 [512, 1024, 384], P(('sub', 'grp')), may hold values from -6 to 6
Outputs:
- solution: float32 [512, 1024, 384], P(('sub', 'grp'))
Inputs may be any that keep to these rules, and one draw needn't show every extreme that they name: `partner`: within the 4 subdomains of one device, the entries form a permutation of 0 to 15. `schur`: each matrix is symmetric positive definite. `coarse_inv`: each matrix is symmetric positive definite.
All inputs are finite; a program needn't handle non-finite values.
Results may differ from a plain program's by a relative error of at most 0.0025.
Values may be sent and summed in bfloat16 or wider, within the bound.
A program may use at most 128 MiB of HBM per device.

v0:
```python
import jax
import jax.numpy as jnp
from jax import lax
from jax.sharding import PartitionSpec as P

ITERS = 2


def shifted(block, axis, distance):
    devices = range(lax.axis_size(axis))
    route = [((i - distance) % len(devices), i) for i in devices]
    return lax.ppermute(block, axis, route)


def face_terms(direction, schur, mortar, partner):
    subdoms = direction.shape[0]
    order = direction.shape[1]
    columns = direction.shape[2]
    faces_all = mortar.shape[1]
    block = mortar.shape[2]
    half_faces = faces_all // 2
    dir_half = direction.astype(jnp.bfloat16)
    stiff = jnp.einsum("sij,sjr->sir", schur, dir_half, preferred_element_type=jnp.float32)
    face_rows = dir_half.reshape(subdoms, faces_all, block, columns)
    traces = jnp.einsum(
        "sfij,sfjr->sfir", mortar, face_rows, preferred_element_type=jnp.float32
    ).astype(jnp.bfloat16)
    upper = traces[:, :half_faces].reshape(subdoms * half_faces, block, columns)
    lower = traces[:, half_faces:].reshape(subdoms * half_faces, block, columns)
    mates = partner.reshape(-1)
    inverse = jnp.argsort(mates)
    reordered = jnp.take(upper, inverse, axis=0)
    lower_mate = shifted(reordered, "sub", 1)
    jump_lower = (lower.astype(jnp.float32) - lower_mate.astype(jnp.float32)).astype(jnp.bfloat16)
    above = shifted(lower, "sub", -1)
    upper_mate = jnp.take(above, mates, axis=0)
    jump_upper = (upper.astype(jnp.float32) - upper_mate.astype(jnp.float32)).astype(jnp.bfloat16)
    jump_all = jnp.concatenate(
        [
            jump_upper.reshape(subdoms, half_faces, block, columns),
            jump_lower.reshape(subdoms, half_faces, block, columns),
        ],
        axis=1,
    )
    pulled = jnp.einsum("sfji,sfjr->sfir", mortar, jump_all, preferred_element_type=jnp.float32)
    return stiff + pulled.reshape(subdoms, order, columns)


def squares(residual):
    return lax.psum(jnp.sum(residual * residual, axis=(0, 1)), ("sub", "grp"))


def on_device(schur, mortar, partner, corner_map, coarse_inv, load):
    order = load.shape[1]
    corner_count = corner_map.shape[1]
    coarse_count = coarse_inv.shape[1]
    stride = order // corner_count
    onehot = (corner_map[..., None] == jnp.arange(coarse_count, dtype=jnp.int32)).astype(
        jnp.float32
    )
    coarse_matrix = coarse_inv[0]
    solution = jnp.zeros_like(load)
    residual = load
    direction = load
    norm_now = squares(residual)
    for step in range(ITERS):
        partial_value = face_terms(direction, schur, mortar, partner)
        corners = direction[:, ::stride, :]
        local_sum = jnp.einsum("sco,scr->or", onehot, corners, precision=lax.Precision.HIGHEST)
        coarse_sum = lax.psum(local_sum.astype(jnp.bfloat16), "grp").astype(jnp.float32)
        coarse_val = jnp.dot(coarse_matrix, coarse_sum, precision=lax.Precision.HIGHEST)
        corner_add = jnp.einsum("sco,or->scr", onehot, coarse_val, precision=lax.Precision.HIGHEST)
        image = partial_value.at[:, ::stride, :].add(corner_add)
        curvature = lax.psum(jnp.sum(direction * image, axis=(0, 1)), ("sub", "grp"))
        image, curvature = (image, curvature)
        step_len = norm_now / curvature
        solution = solution + step_len * direction
        if step + 1 < ITERS:
            residual = residual - step_len * image
            norm_next = squares(residual)
            direction = residual + norm_next / norm_now * direction
            norm_now = norm_next
    return solution


def solution(mesh):
    return jax.shard_map(
        on_device,
        mesh=mesh,
        in_specs=(
            P(("sub", "grp"), None, None),
            P(("sub", "grp"), None, None, None),
            P(("sub", "grp"), None),
            P(("sub", "grp"), None),
            P("sub", None, None),
            P(("sub", "grp"), None, None),
        ),
        out_specs=P(("sub", "grp"), None, None),
        check_vma=False,
    )
```

profile of v0, /device:TPU:1, one launch (start us, length us, event | category | flops | bytes accessed | tf_op | source)
XLA Modules:
  0.0 520.1 jit_solution(5917532602240920158)
XLA Ops:
  6.5 5.6 %multiply_reduce_fusion.1 = (f32[384]{0:T(512)S(1)}, bf16[4,1024,384]{2,1,0:T(8,128)(2,1)S(1)}) fusion(f32[4,1024,384]{2,1,0:T(8,128)} %param.13), kind=kLoop, calls=%fused_computation.17 | loop fusion | flops 4718208 | bytes 9438720 | tf_op jit(solution)/shard_map/reduce_sum | solution.py:50
  20.0 2.8 broadcast_select_fusion.1
  24.4 2.8 slice.20
  28.6 82.6 %all-reduce.4.cloned.1.call-done = bf16[128,384]{1,0:T(8,128)(2,1)} async-done(((bf16[128,384]{1,0:T(8,128)(2,1)}), bf16[128,384]{1,0:T(8,128)(2,1)}) %all-reduce.4.cloned.1.call-update) | async-done | bytes 98320 | tf_op jit(solution)/shard_map/psum | solution.py:70
  112.7 3.3 gather_fusion
  116.0 2.1 subtract_convert_fusion.3
  118.2 2.5 subtract_convert_fusion.2
  123.9 6.9 %bitcast_add_fusion = f32[4,1024,384]{2,1,0:T(8,128)} fusion(f32[4,8,384,128]{2,3,1,0:T(8,128)S(1)} %fusion.3, bf16[4,1024,1024]{2,1,0:T(8,128)(2,1)S(1)} %bitcast.65, bf16[4,1024,384]{2,1,0:T(8,128)(2,1)S(1)} %copy-done.2), kind=kOutput, calls=%fused_computation.6 | convolution fusion | flops 3222798336 | bytes 24117248 | tf_op jit(solution)/shard_map/sij,sjr->sir/dot_general | solution.py:23
  130.8 9.5 %copy.24 = f32[4,1024,384]{2,0,1:T(4,128)} copy(f32[4,1024,384]{2,1,0:T(8,128)} %bitcast_add_fusion) | data formatting | bytes 12582912 | tf_op jit(solution)/shard_map/add | solution.py:46
  140.3 2.1 scatter_fusion
  142.4 9.6 %fusion.2 = f32[384]{0:T(512)S(1)} fusion(f32[4,1024,384]{2,0,1:T(4,128)} %scatter_fusion, f32[4,1024,384]{2,1,0:T(8,128)} %param.13), kind=kLoop, calls=%fused_computation.13 | loop fusion | flops 3145344 | bytes 12584448 | tf_op jit(solution)/shard_map/reduce_sum | solution.py:74
  152.0 64.9 %all-reduce = (f32[384]{0:T(512)S(1)}, f32[384]{0:T(512)S(1)}) all-reduce(f32[384]{0:T(512)S(1)} %get-tuple-element.12, f32[384]{0:T(512)S(1)} %fusion.2), channel_id=1, replica_groups=mesh['sub'=8,'grp'=16] {'sub','grp'}, use_global_device_ids=true, to_apply=%region_1.0 | all-reduce | flops 768 | bytes 6144 | tf_op jit(solution)/shard_map/psum | solution.py:50
  216.9 5.5 %multiply_reduce_fusion = f32[384]{0:T(512)S(1)} fusion(f32[4,1024,384]{2,1,0:T(8,128)} %param.13, f32[4,1024,384]{2,0,1:T(4,128)} %scatter_fusion, f32[384]{0:T(512)S(1)} %div.9), kind=kLoop, calls=%fused_computation.16 | loop fusion | flops 6291072 | bytes 12585984 | tf_op jit(solution)/shard_map/reduce_sum | solution.py:50
  222.4 64.4 %psum.45 = f32[384]{0:T(512)S(1)} all-reduce(f32[384]{0:T(512)S(1)} %multiply_reduce_fusion), channel_id=1, replica_groups=mesh['sub'=8,'grp'=16] {'sub','grp'}, use_global_device_ids=true, to_apply=%region_8.10 | all-reduce | flops 384 | bytes 3072 | tf_op jit(solution)/shard_map/psum | solution.py:50
  286.8 7.1 %fusion.21 = (bf16[4,1024,384]{2,1,0:T(8,128)(2,1)S(1)}, f32[4,1024,384]{2,1,0:T(8,128)}) fusion(f32[4,1024,384]{2,1,0:T(8,128)} %param.13, f32[384]{0:T(512)S(1)} %div.10, f32[4,1024,384]{2,0,1:T(4,128)} %scatter_fusion, f32[384]{0:T(512)S(1)} %div.9), kind=kLoop, calls=%fused_computation.58 | loop fusion | flops 7864320 | bytes 22023168 | tf_op jit(solution)/shard_map/convert_element_type | solution.py:22
  297.0 1.9 gather_fusion.3
  298.9 2.8 broadcast_select_fusion
  302.7 2.8 slice.23
  306.5 78.2 %all-reduce.6.cloned.1.call-done = bf16[128,384]{1,0:T(8,128)(2,1)} async-done(((bf16[128,384]{1,0:T(8,128)(2,1)}), bf16[128,384]{1,0:T(8,128)(2,1)}) %all-reduce.6.cloned.1.call-update) | async-done | bytes 98320 | tf_op jit(solution)/shard_map/psum | solution.py:70
  386.1 3.5 subtract_convert_fusion
  389.6 2.6 copy.31
  392.2 3.3 gather_fusion.2
  395.5 3.1 subtract_convert_fusion.1
  398.7 2.7 copy.30
  401.3 5.1 fusion.7
  406.4 6.5 %copy.41 = f32[4,1024,384]{1,2,0:T(8,128)} copy(f32[4,1024,384]{2,1,0:T(8,128)} %bitcast.68) | data formatting | bytes 12582912 | tf_op jit(solution)/shard_map/reshape | solution.py:46
  413.0 12.4 %bitcast_add_fusion.1 = f32[4,1024,384]{1,2,0:T(8,128)} fusion(f32[4,1024,384]{1,2,0:T(8,128)} %copy.41, bf16[4,1024,384]{2,1,0:T(8,128)(2,1)} %copy-done.3, bf16[4,1024,1024]{2,1,0:T(8,128)(2,1)} %param.8), kind=kOutput, calls=%fused_computation.7 | convolution fusion | flops 3222798336 | bytes 24117248 | tf_op jit(solution)/shard_map/sij,sjr->sir/dot_general | solution.py:23
  425.3 7.7 %copy.34 = f32[4,1024,384]{2,0,1:T(4,128)} copy(f32[4,1024,384]{1,2,0:T(8,128)} %bitcast_add_fusion.1) | data formatting | bytes 12582912 | tf_op jit(solution)/shard_map/add | solution.py:46
  433.0 2.1 scatter_fusion.1
  435.1 5.3 %fusion = f32[384]{0:T(512)S(1)} fusion(f32[4,1024,384]{2,1,0:T(8,128)} %get-tuple-element.11, f32[4,1024,384]{2,0,1:T(4,128)} %scatter_fusion.1), kind=kLoop, calls=%fused_computation.9 | loop fusion | flops 3145344 | bytes 12584448 | tf_op jit(solution)/shard_map/reduce_sum | solution.py:74
  440.3 64.9 %psum.47 = f32[384]{0:T(512)S(1)} all-reduce(f32[384]{0:T(512)S(1)} %fusion), channel_id=1, replica_groups=mesh['sub'=8,'grp'=16] {'sub','grp'}, use_global_device_ids=true, to_apply=%region_12.14 | all-reduce | flops 384 | bytes 3072 | tf_op jit(solution)/shard_map/psum | solution.py:74
  505.2 8.0 %multiply_add_fusion = f32[4,1024,384]{2,1,0:T(8,128)} fusion(f32[4,1024,384]{2,1,0:T(8,128)} %get-tuple-element.11, f32[4,1024,384]{2,1,0:T(8,128)} %param.13, f32[384]{0:T(512)S(1)} %div.11, f32[384]{0:T(512)S(1)} %div.9), kind=kLoop, calls=%fused_computation.14 | loop fusion | flops 4718592 | bytes 18877440 | tf_op jit(solution)/shard_map/add | solution.py:77
  (60 shorter events, 21.9 us)
Async XLA Ops:
  6.5 5.6 %copy-start = (bf16[4,8,128,128]{3,2,1,0:T(8,128)(2,1)S(1)}, bf16[4,8,128,128]{3,2,1,0:T(8,128)(2,1)}, u32[]{:S(2)}) copy-start(bf16[4,8,128,128]{3,2,1,0:T(8,128)(2,1)} %param.9) | copy-start | bytes 3145732
  6.5 104.7 %all-reduce.4.cloned.1.call-start = ((), (), s32[]{:S(2)}) async-start(), calls=%async_computation | async-start | bytes 196608 | tf_op jit(solution)/shard_map/psum | solution.py:70
  12.2 1.7 copy-start.1
  13.8 3.0 copy-start.7
  15.4 97.3 %collective-permute-start = (bf16[16,128,384]{2,1,0:T(8,128)(2,1)}, bf16[16,128,384]{2,1,0:T(8,128)(2,1)}, u32[]{:S(2)}, u32[]{:S(2)}) collective-permute-start(bf16[16,128,384]{2,1,0:T(8,128)(2,1)} %bitcast.2), channel_id=1, source_target_pairs={{16,0},{32,16},{48,32},{64,48},{80,64},{96,80},{112,96},{0,112},{1... | collective-permute-start | bytes 4718600 | tf_op jit(solution)/shard_map/ppermute | solution.py:12
  18.1 9.2 %copy-start.6 = (s32[4,8]{1,0:T(4,128)S(1)}, s32[4,8]{1,0:T(4,128)}, u32[]{:S(2)}) copy-start(s32[4,8]{1,0:T(4,128)} %param.11) | copy-start | bytes 388
  18.1 93.1 %copy-start.5 = (f32[1,128,128]{2,1,0:T(8,128)S(1)}, f32[1,128,128]{2,1,0:T(8,128)}, u32[]{:S(2)}) copy-start(f32[1,128,128]{2,1,0:T(8,128)} %param.12) | copy-start | bytes 196612
  22.8 95.3 %collective-permute-start.1 = (bf16[16,128,384]{2,1,0:T(8,128)(2,1)}, bf16[16,128,384]{2,1,0:T(8,128)(2,1)}, u32[]{:S(2)}, u32[]{:S(2)}) collective-permute-start(bf16[16,128,384]{2,1,0:T(8,128)(2,1)} %broadcast_select_fusion.1), channel_id=1, source_target_pairs={{112,0},{0,16},{16,32},{32,48},{48,64},{64,80},{80,96},{96,112},{1... | collective-permute-start | bytes 4718600 | tf_op jit(solution)/shard_map/ppermute | solution.py:12
  28.3 356.4 %all-reduce.6.cloned.1.call-start = ((), (), s32[]{:S(2)}) async-start(), calls=%async_computation.1 | async-start | bytes 196608 | tf_op jit(solution)/shard_map/psum | solution.py:70
  118.2 3.6 slice-start
  120.7 2.3 slice-start.1
  120.7 3.2 copy-start.2
  293.9 1.7 copy-start.3
  301.7 84.4 %collective-permute-start.3 = (bf16[16,128,384]{1,2,0:T(8,128)(2,1)}, bf16[16,128,384]{1,2,0:T(8,128)(2,1)}, u32[]{:S(2)}, u32[]{:S(2)}) collective-permute-start(bf16[16,128,384]{1,2,0:T(8,128)(2,1)} %broadcast_select_fusion), channel_id=1, source_target_pairs={{112,0},{0,16},{16,32},{32,48},{48,64},{64,80},{80,96},{96,112},{1... | collective-permute-start | bytes 4718600 | tf_op jit(solution)/shard_map/ppermute | solution.py:12
  301.7 90.5 %collective-permute-start.2 = (bf16[16,128,384]{1,2,0:T(8,128)(2,1)}, bf16[16,128,384]{1,2,0:T(8,128)(2,1)}, u32[]{:S(2)}, u32[]{:S(2)}) collective-permute-start(bf16[16,128,384]{1,2,0:T(8,128)(2,1)} %bitcast.16), channel_id=1, source_target_pairs={{16,0},{32,16},{48,32},{64,48},{80,64},{96,80},{112,96},{0,112},{1... | collective-permute-start | bytes 4718600 | tf_op jit(solution)/shard_map/ppermute | solution.py:12
  398.7 2.7 copy-start.4
Sparse Core Ops, SparseCore 0:
  28.4 82.7 all-reduce.3
  306.6 77.9 all-reduce.5
where the time goes:
time: 521 us; the launch traced here: 520 us
  blocking collectives  194 us (37%)
  waiting for transfers between devices  161 us (31%)
  other arithmetic  63.4 us (12%)
  local copies, waits for them, and re-layouts  51.5 us (10%)
  matrix products  32.3 us (6%)
  between operations  13.6 us (3%)
    psum x2, waiting for transfers between devices, on_device(): lax.psum(local_sum.astype(jnp.bfloat16), 'grp').astype(jnp.float32)  161 us
    psum x2, blocking collectives, squares(): return lax.psum(jnp.sum(residual * residual, axis=(0, 1)), ('sub', 'grp'))  129 us
    psum x1, blocking collectives, on_device(): lax.psum(jnp.sum(direction * image, axis=(0, 1)), ('sub', 'grp'))  64.9 us
    dot_general x2, matrix products, face_terms(): jnp.einsum('sij,sjr->sir', schur, dir_half, preferred_element_type=jnp.fl...  19.3 us
    add x2, local copies, waits for them, and re-layouts, face_terms(): return stiff + pulled.reshape(subdoms, order, columns)  17.1 us
    reduce_sum x2, other arithmetic, on_device(): jnp.sum(direction * image, axis=(0, 1))  14.9 us
    reduce_sum x2, other arithmetic, squares(): return lax.psum(jnp.sum(residual * residual, axis=(0, 1)), ('sub', 'grp'))  11.1 us
  transfers between devices with their start and end apart: 6, of which 2 were waited for; matrix products, arithmetic and copies ran while one was open for 5% of the time, Pallas kernels for 0%

commit v1 on v0

--- a/solution.py
+++ b/solution.py
@@ -47,7 +47,7 @@
 
 
 def squares(residual):
-    return lax.psum(jnp.sum(residual * residual, axis=(0, 1)), ("sub", "grp"))
+    return lax.psum(lax.psum(jnp.sum(residual * residual, axis=(0, 1)), "grp"), "sub")
 
 
 def on_device(schur, mortar, partner, corner_map, coarse_inv, load):

time: 521 us -> 505 us (0.969)
  waiting for transfers between devices: 161 us -> 104 us
  blocking collectives: 194 us -> 235 us
    psum x1 -> x2, blocking collectives: 64.9 us -> 130 us  [on_device(): lax.psum(jnp.sum(direction * image, axis=(0, 1)), ('sub', 'grp'))]
    psum x2, waiting for transfers between devices: 161 us -> 104 us  [on_device(): lax.psum(local_sum.astype(jnp.bfloat16), 'grp').astype(jnp.float32)]
    psum x2 -> x4, blocking collectives: 129 us -> 105 us  [the longest x2 64.6 us: squares(): lax.psum(jnp.sum(residual * residual, axis=(0, 1)), 'grp')]
  transfers between devices with their start and end apart: 6 -> 6, of which waited for: 2 -> 2; matrix products, arithmetic and copies ran while one was open for 5% -> 6% of each run, Pallas kernels for 0% -> 0%
where the time goes in v1:
time: 505 us; the launch traced here: 504 us
  blocking collectives  235 us (47%)
  waiting for transfers between devices  104 us (21%)
  other arithmetic  63.4 us (13%)
  local copies, waits for them, and re-layouts  51.5 us (10%)
  matrix products  32.3 us (6%)
  between operations  13.6 us (3%)
    psum x2, blocking collectives, on_device(): lax.psum(jnp.sum(direction * image, axis=(0, 1)), ('sub', 'grp'))  130 us
    psum x2, waiting for transfers between devices, on_device(): lax.psum(local_sum.astype(jnp.bfloat16), 'grp').astype(jnp.float32)  104 us
    psum x2, blocking collectives, squares(): lax.psum(jnp.sum(residual * residual, axis=(0, 1)), 'grp')  64.6 us
    psum x2, blocking collectives, squares(): lax.psum(lax.psum(jnp.sum(residual * residual, axis=(0, 1)), 'grp'), 'sub')  40.7 us
    dot_general x2, matrix products, face_terms(): jnp.einsum('sij,sjr->sir', schur, dir_half, preferred_element_type=jnp.fl...  19.3 us
    add x2, local copies, waits for them, and re-layouts, face_terms(): return stiff + pulled.reshape(subdoms, order, columns)  17.1 us
    reduce_sum x2, other arithmetic, on_device(): jnp.sum(direction * image, axis=(0, 1))  14.9 us
    reduce_sum x2, other arithmetic, squares(): jnp.sum(residual * residual, axis=(0, 1))  11.1 us
  transfers between devices with their start and end apart: 6, of which 2 were waited for; matrix products, arithmetic and copies ran while one was open for 6% of the time, Pallas kernels for 0%

profile of v1, /device:TPU:1, one launch (start us, length us, event | category | flops | bytes accessed | tf_op | source)
XLA Modules:
  0.0 504.1 jit_solution(4005059461558735041)
XLA Ops:
  6.5 5.6 %multiply_reduce_fusion.1 = (f32[384]{0:T(512)S(1)}, bf16[4,1024,384]{2,1,0:T(8,128)(2,1)S(1)}) fusion(f32[4,1024,384]{2,1,0:T(8,128)} %param.13), kind=kLoop, calls=%fused_computation.17 | loop fusion | flops 4718208 | bytes 9438720 | tf_op jit(solution)/shard_map/reduce_sum | solution.py:50
  20.0 2.8 broadcast_select_fusion.1
  24.4 2.8 slice.20
  28.3 33.8 %psum.56 = f32[384]{0:T(512)S(1)} all-reduce(f32[384]{0:T(512)S(1)} %get-tuple-element.10), channel_id=1, replica_groups=mesh['sub'=8,'grp'=16] {'grp'}, use_global_device_ids=true, to_apply=%region_1.0 | all-reduce | flops 384 | bytes 3072 | tf_op jit(solution)/shard_map/psum | solution.py:50
  62.1 20.9 %psum.57 = f32[384]{0:T(512)S(1)} all-reduce(f32[384]{0:T(512)S(1)} %psum.56), channel_id=1, replica_groups=mesh['sub'=8,'grp'=16] {'sub'}, use_global_device_ids=true, to_apply=%region_2.0 | all-reduce | flops 384 | bytes 3072 | tf_op jit(solution)/shard_map/psum | solution.py:50
  83.0 28.2 %all-reduce.3.cloned.1.call-done = bf16[128,384]{1,0:T(8,128)(2,1)} async-done(((bf16[128,384]{1,0:T(8,128)(2,1)}), bf16[128,384]{1,0:T(8,128)(2,1)}) %all-reduce.3.cloned.1.call-update) | async-done | bytes 98320 | tf_op jit(solution)/shard_map/psum | solution.py:70
  112.7 3.3 gather_fusion
  116.0 2.1 subtract_convert_fusion.3
  118.2 2.5 subtract_convert_fusion.2
  123.9 6.9 %bitcast_add_fusion = f32[4,1024,384]{2,1,0:T(8,128)} fusion(f32[4,8,384,128]{2,3,1,0:T(8,128)S(1)} %fusion.3, bf16[4,1024,1024]{2,1,0:T(8,128)(2,1)S(1)} %bitcast.65, bf16[4,1024,384]{2,1,0:T(8,128)(2,1)S(1)} %copy-done.2), kind=kOutput, calls=%fused_computation.6 | convolution fusion | flops 3222798336 | bytes 24117248 | tf_op jit(solution)/shard_map/sij,sjr->sir/dot_general | solution.py:23
  130.9 9.5 %copy.24 = f32[4,1024,384]{2,0,1:T(4,128)} copy(f32[4,1024,384]{2,1,0:T(8,128)} %bitcast_add_fusion) | data formatting | bytes 12582912 | tf_op jit(solution)/shard_map/add | solution.py:46
  142.4 9.6 %fusion.2 = f32[384]{0:T(512)S(1)} fusion(f32[4,1024,384]{2,0,1:T(4,128)} %scatter_fusion, f32[4,1024,384]{2,1,0:T(8,128)} %param.13), kind=kLoop, calls=%fused_computation.13 | loop fusion | flops 3145344 | bytes 12584448 | tf_op jit(solution)/shard_map/reduce_sum | solution.py:74
  152.0 64.9 %psum.59 = f32[384]{0:T(512)S(1)} all-reduce(f32[384]{0:T(512)S(1)} %fusion.2), channel_id=1, replica_groups=mesh['sub'=8,'grp'=16] {'sub','grp'}, use_global_device_ids=true, to_apply=%region_7.9 | all-reduce | flops 384 | bytes 3072 | tf_op jit(solution)/shard_map/psum | solution.py:74
  216.9 5.5 %multiply_reduce_fusion = f32[384]{0:T(512)S(1)} fusion(f32[4,1024,384]{2,1,0:T(8,128)} %param.13, f32[4,1024,384]{2,0,1:T(4,128)} %scatter_fusion, f32[384]{0:T(512)S(1)} %div.9), kind=kLoop, calls=%fused_computation.16 | loop fusion | flops 6291072 | bytes 12585984 | tf_op jit(solution)/shard_map/reduce_sum | solution.py:50
  222.5 30.8 %psum.60 = f32[384]{0:T(512)S(1)} all-reduce(f32[384]{0:T(512)S(1)} %multiply_reduce_fusion), channel_id=1, replica_groups=mesh['sub'=8,'grp'=16] {'grp'}, use_global_device_ids=true, to_apply=%region_9.11 | all-reduce | flops 384 | bytes 3072 | tf_op jit(solution)/shard_map/psum | solution.py:50
  253.3 19.8 %psum.61 = f32[384]{0:T(512)S(1)} all-reduce(f32[384]{0:T(512)S(1)} %psum.60), channel_id=1, replica_groups=mesh['sub'=8,'grp'=16] {'sub'}, use_global_device_ids=true, to_apply=%region_10.12 | all-reduce | flops 384 | bytes 3072 | tf_op jit(solution)/shard_map/psum | solution.py:50
  273.1 7.1 %fusion.21 = (bf16[4,1024,384]{2,1,0:T(8,128)(2,1)S(1)}, f32[4,1024,384]{2,1,0:T(8,128)}) fusion(f32[4,1024,384]{2,1,0:T(8,128)} %param.13, f32[384]{0:T(512)S(1)} %div.10, f32[4,1024,384]{2,0,1:T(4,128)} %scatter_fusion, f32[384]{0:T(512)S(1)} %div.9), kind=kLoop, calls=%fused_computation.58 | loop fusion | flops 7864320 | bytes 22023168 | tf_op jit(solution)/shard_map/convert_element_type | solution.py:22
  285.2 2.8 broadcast_select_fusion
  288.9 2.8 slice.23
  292.8 75.9 %all-reduce.5.cloned.1.call-done = bf16[128,384]{1,0:T(8,128)(2,1)} async-done(((bf16[128,384]{1,0:T(8,128)(2,1)}), bf16[128,384]{1,0:T(8,128)(2,1)}) %all-reduce.5.cloned.1.call-update) | async-done | bytes 98320 | tf_op jit(solution)/shard_map/psum | solution.py:70
  370.2 3.5 subtract_convert_fusion
  373.7 2.6 copy.31
  376.2 3.3 gather_fusion.2
  379.6 3.1 subtract_convert_fusion.1
  382.7 2.7 copy.30
  385.4 5.1 %fusion.7 = f32[4,8,384,128]{2,3,1,0:T(8,128)} fusion(bf16[4,8,128,128]{3,2,1,0:T(8,128)(2,1)S(1)} %copy-done, bf16[4,4,128,384]{3,2,1,0:T(8,128)(2,1)S(1)} %bitcast.72, bf16[4,4,128,384]{3,2,1,0:T(8,128)(2,1)} %bitcast.74), kind=kOutput, calls=%fused_computation.22 | convolution fusion | flops 404226048 | bytes 10485760 | tf_op jit(solution)/shard_map/sfji,sfjr->sfir/dot_general | solution.py:45
  390.5 6.5 %copy.41 = f32[4,1024,384]{1,2,0:T(8,128)} copy(f32[4,1024,384]{2,1,0:T(8,128)} %bitcast.68) | data formatting | bytes 12582912 | tf_op jit(solution)/shard_map/reshape | solution.py:46
  397.0 12.4 %bitcast_add_fusion.1 = f32[4,1024,384]{1,2,0:T(8,128)} fusion(f32[4,1024,384]{1,2,0:T(8,128)} %copy.41, bf16[4,1024,384]{2,1,0:T(8,128)(2,1)} %copy-done.3, bf16[4,1024,1024]{2,1,0:T(8,128)(2,1)} %param.8), kind=kOutput, calls=%fused_computation.7 | convolution fusion | flops 3222798336 | bytes 24117248 | tf_op jit(solution)/shard_map/sij,sjr->sir/dot_general | solution.py:23
  409.4 7.7 %copy.34 = f32[4,1024,384]{2,0,1:T(4,128)} copy(f32[4,1024,384]{1,2,0:T(8,128)} %bitcast_add_fusion.1) | data formatting | bytes 12582912 | tf_op jit(solution)/shard_map/add | solution.py:46
  419.1 5.3 %fusion = f32[384]{0:T(512)S(1)} fusion(f32[4,1024,384]{2,1,0:T(8,128)} %get-tuple-element.9, f32[4,1024,384]{2,0,1:T(4,128)} %scatter_fusion.1), kind=kLoop, calls=%fused_computation.9 | loop fusion | flops 3145344 | bytes 12584448 | tf_op jit(solution)/shard_map/reduce_sum | solution.py:74
  424.4 64.9 %psum.63 = f32[384]{0:T(512)S(1)} all-reduce(f32[384]{0:T(512)S(1)} %fusion), channel_id=1, replica_groups=mesh['sub'=8,'grp'=16] {'sub','grp'}, use_global_device_ids=true, to_apply=%region_14.16 | all-reduce | flops 384 | bytes 3072 | tf_op jit(solution)/shard_map/psum | solution.py:74
  489.3 8.0 %multiply_add_fusion = f32[4,1024,384]{2,1,0:T(8,128)} fusion(f32[4,1024,384]{2,1,0:T(8,128)} %get-tuple-element.9, f32[4,1024,384]{2,1,0:T(8,128)} %param.13, f32[384]{0:T(512)S(1)} %div.11, f32[384]{0:T(512)S(1)} %div.9), kind=kLoop, calls=%fused_computation.14 | loop fusion | flops 4718592 | bytes 18877440 | tf_op jit(solution)/shard_map/add | solution.py:77
  (63 shorter events, 27.7 us)
Async XLA Ops:
  6.5 5.6 %copy-start = (bf16[4,8,128,128]{3,2,1,0:T(8,128)(2,1)S(1)}, bf16[4,8,128,128]{3,2,1,0:T(8,128)(2,1)}, u32[]{:S(2)}) copy-start(bf16[4,8,128,128]{3,2,1,0:T(8,128)(2,1)} %param.9) | copy-start | bytes 3145732
  6.5 104.7 %all-reduce.3.cloned.1.call-start = ((), (), s32[]{:S(2)}) async-start(), calls=%async_computation | async-start | bytes 196608 | tf_op jit(solution)/shard_map/psum | solution.py:70
  12.2 1.7 copy-start.1
  13.8 3.0 copy-start.7
  15.4 97.3 %collective-permute-start = (bf16[16,128,384]{2,1,0:T(8,128)(2,1)}, bf16[16,128,384]{2,1,0:T(8,128)(2,1)}, u32[]{:S(2)}, u32[]{:S(2)}) collective-permute-start(bf16[16,128,384]{2,1,0:T(8,128)(2,1)} %bitcast.2), channel_id=1, source_target_pairs={{16,0},{32,16},{48,32},{64,48},{80,64},{96,80},{112,96},{0,112},{1... | collective-permute-start | bytes 4718600 | tf_op jit(solution)/shard_map/ppermute | solution.py:12
  18.1 9.2 %copy-start.6 = (s32[4,8]{1,0:T(4,128)S(1)}, s32[4,8]{1,0:T(4,128)}, u32[]{:S(2)}) copy-start(s32[4,8]{1,0:T(4,128)} %param.11) | copy-start | bytes 388
  18.1 93.1 %copy-start.5 = (f32[1,128,128]{2,1,0:T(8,128)S(1)}, f32[1,128,128]{2,1,0:T(8,128)}, u32[]{:S(2)}) copy-start(f32[1,128,128]{2,1,0:T(8,128)} %param.12) | copy-start | bytes 196612
  22.8 95.3 %collective-permute-start.1 = (bf16[16,128,384]{2,1,0:T(8,128)(2,1)}, bf16[16,128,384]{2,1,0:T(8,128)(2,1)}, u32[]{:S(2)}, u32[]{:S(2)}) collective-permute-start(bf16[16,128,384]{2,1,0:T(8,128)(2,1)} %broadcast_select_fusion.1), channel_id=1, source_target_pairs={{112,0},{0,16},{16,32},{32,48},{48,64},{64,80},{80,96},{96,112},{1... | collective-permute-start | bytes 4718600 | tf_op jit(solution)/shard_map/ppermute | solution.py:12
  28.3 340.4 %all-reduce.5.cloned.1.call-start = ((), (), s32[]{:S(2)}) async-start(), calls=%async_computation.1 | async-start | bytes 196608 | tf_op jit(solution)/shard_map/psum | solution.py:70
  118.2 3.6 slice-start
  120.7 2.3 slice-start.1
  120.7 3.2 copy-start.2
  280.3 1.7 copy-start.3
  288.0 82.2 %collective-permute-start.3 = (bf16[16,128,384]{1,2,0:T(8,128)(2,1)}, bf16[16,128,384]{1,2,0:T(8,128)(2,1)}, u32[]{:S(2)}, u32[]{:S(2)}) collective-permute-start(bf16[16,128,384]{1,2,0:T(8,128)(2,1)} %broadcast_select_fusion), channel_id=1, source_target_pairs={{112,0},{0,16},{16,32},{32,48},{48,64},{64,80},{80,96},{96,112},{1... | collective-permute-start | bytes 4718600 | tf_op jit(solution)/shard_map/ppermute | solution.py:12
  288.0 88.2 %collective-permute-start.2 = (bf16[16,128,384]{1,2,0:T(8,128)(2,1)}, bf16[16,128,384]{1,2,0:T(8,128)(2,1)}, u32[]{:S(2)}, u32[]{:S(2)}) collective-permute-start(bf16[16,128,384]{1,2,0:T(8,128)(2,1)} %bitcast.16), channel_id=1, source_target_pairs={{16,0},{32,16},{48,32},{64,48},{80,64},{96,80},{112,96},{0,112},{1... | collective-permute-start | bytes 4718600 | tf_op jit(solution)/shard_map/ppermute | solution.py:12
  382.7 2.7 copy-start.4
Sparse Core Ops, SparseCore 0:
  28.4 82.7 all-reduce.2
  292.9 75.7 all-reduce.4
